TPU v7x, 32 devices: a whole 2x2x4 slice. The times are simulated.
32 devices in a mesh: group: 4 (over x, core), tile: 8 (over z, y).
Axes of the slice: x: 2, y: 2, z: 4, core: 2. Of those that a mesh axis runs over, the one named last changes fastest.
Arguments:
- object_slices: bfloat16 [4, 2048, 1024], P(None, 'group', 'tile'), may hold values from -4 to 4
- probe: float32 [1024, 256], replicated, may hold values from -6 to 6
- mid_waves: bfloat16 [4, 8, 3, 2, 2, 256, 256], P('group', 'tile'), may hold values from -160 to 160
- amplitudes: bfloat16 [4, 8, 3, 256, 256], P('group', 'tile'), may hold values from 0.19921875 to 4
- row_offsets: int32 [4, 8, 3], P('group', 'tile'), may hold values from 0 to 256
- col_offsets: int32 [4, 8, 3], P('group', 'tile'), may hold values from 0 to 128
Outputs:
- object_new: float32 [4, 2048, 1024], P(None, 'group', 'tile')
- probe_new: float32 [1024, 256], P('tile')
All inputs are finite; a program needn't handle non-finite values.
Results may differ from a plain program's by a relative error of at most 0.0003.
Values may be sent and summed in bfloat16 or wider, within the bound.
No kernel may reach another device: no remote copies, remote signals or barrier semaphores. Data moves between devices by JAX's collectives and lax.ppermute only.
A program may use at most 128 MiB of HBM per device.

v0:
```python
import jax
import jax.numpy as jnp
import numpy as np
from jax import lax
from jax.experimental import pallas as pl
from jax.experimental.pallas import tpu as pltpu
from jax.sharding import PartitionSpec as P

phase_rate = 0.25
floor_level = 0.5
object_step = 0.5
probe_step = 0.5
epsilon = 1e-06
object_bound = 4.0
amp_bound = 4.0
half_range = 32768.0

F32 = jnp.float32
BF16 = jnp.bfloat16
whole_vmem = pl.BlockSpec(memory_space=pltpu.VMEM)
whole_smem = pl.BlockSpec(memory_space=pltpu.SMEM)


def hi_lo(table):
    table = np.asarray(table, np.float64)
    high = table.astype(np.float32).astype(BF16)
    low = (table - high.astype(np.float64)).astype(np.float32).astype(BF16)
    return np.stack([high, low])


def complex_block(real, imag):
    return np.block([[real, -imag], [imag, real]])


def dft_tables(size):
    half = size // 2
    index = np.arange(half)
    norming = 1.0 / np.sqrt(size)
    tables = []
    for parity in (0, 1):
        angle = 2.0 * np.pi * (np.outer(2 * index + parity, index) % size) / size
        cos, sin = np.cos(angle) * norming, np.sin(angle) * norming
        tables.append(hi_lo(complex_block(cos, -sin)))
        tables.append(hi_lo(complex_block(cos.T, sin.T)))
    left_even, right_even, left_odd, right_odd = tables
    return np.stack([left_even, left_odd, right_even, right_odd])


def back_tables(size):
    half = size // 2
    freq = np.fft.fftfreq(size, 1.0 / size)
    row = np.fft.ifft(np.exp(1j * 2.0 * np.pi * phase_rate / size * freq * freq))
    shift = np.arange(half)[:, None] - np.arange(half)[None, :]
    same, cross = row[shift % size], row[(shift + half) % size]
    even, odd = 0.5 * (same + cross), 0.5 * (same - cross)
    left = [hi_lo(complex_block(part.real, part.imag)) for part in (even, odd)]
    right = [hi_lo(complex_block(part.real, -part.imag)) for part in (even, odd)]
    return np.stack(left + right)


def order_table(size):
    order = np.concatenate([np.arange(0, size, 2), np.arange(1, size, 2)])
    table = np.zeros((size, size), np.float32)
    table[np.arange(size), order] = 1.0
    return np.stack([table, table.T]).astype(BF16)


def dot(left, right):
    return jnp.dot(left, right, preferred_element_type=F32)


def split(value):
    high = value.astype(BF16)
    return high, (value - high.astype(F32)).astype(BF16)


def from_left(table, which, value):
    high, low = split(value)
    return (
        dot(table[which, 0], high) + dot(table[which, 0], low) + dot(table[which, 1], high)
    )


def from_right(value, table, which):
    high, low = split(value)
    return (
        dot(high, table[which, 0]) + dot(low, table[which, 0]) + dot(high, table[which, 1])
    )


def join(parts, axis):
    return jnp.concatenate(parts, axis=axis)


def fold_rows(fields):
    half = fields[0][0].shape[0] // 2
    plus = join([join([part[:half] + part[half:] for part in f], 0) for f in fields], 1)
    minus = join([join([part[:half] - part[half:] for part in f], 0) for f in fields], 1)
    return plus, minus


def fold_lanes(first, second, count):
    half = first.shape[0] // 2
    width = first.shape[1] // count
    plus, minus = [], []
    for mode in range(count):
        for array in (first, second):
            a = array[:, mode * width : mode * width + width // 2]
            b = array[:, mode * width + width // 2 : (mode + 1) * width]
            s, d = a + b, a - b
            plus.append(join([s[:half], s[half:]], 1))
            minus.append(join([d[:half], d[half:]], 1))
    return join(plus, 0), join(minus, 0)


def unfold_lanes(even, odd, count):
    low, high = even + odd, even - odd
    half = even.shape[1] // 2
    arrays = []
    for which in range(2):
        modes = []
        for mode in range(count):
            rows = slice((2 * mode + which) * half, (2 * mode + which + 1) * half)
            x0, x1 = low[rows], high[rows]
            modes.append(
                join([join([x0[:, :half], x1[:, :half]], 1), join([x0[:, half:], x1[:, half:]], 1)], 0)
            )
        arrays.append(join(modes, 1))
    return arrays


def unfold_rows(even, odd, count):
    top, bottom = even + odd, even - odd
    half = even.shape[0] // 2
    width = even.shape[1] // count
    fields = []
    for mode in range(count):
        cols = slice(mode * width, (mode + 1) * width)
        fields.append(
            (
                join([top[:half, cols], bottom[:half, cols]], 0),
                join([top[half:, cols], bottom[half:, cols]], 0),
            )
        )
    return fields


def masks(row_at, col_at, size, width):
    low_rows = lax.broadcasted_iota(jnp.int32, (size, width), 0) >= row_at
    left_cols = lax.broadcasted_iota(jnp.int32, (size, width), 1) >= col_at
    return low_rows, left_cols


def patch_of(left, own, right, part, low_rows, left_cols):
    size = low_rows.shape[0]

    def rows_of(ref):
        return jnp.where(low_rows, ref[part, :size].astype(F32), ref[part, size:].astype(F32))

    halo = jnp.where(left_cols, rows_of(left), rows_of(right))
    return join([halo, rows_of(own)], 1)


def scatter(part, value, scale, left, own, right, low_rows, left_cols):
    size, width = low_rows.shape
    halo, mine = value[:, :width] * scale, value[:, width:]
    zero = jnp.zeros_like(halo)
    to_left = jnp.where(left_cols, halo, zero)
    to_right = halo - to_left
    for ref, term in ((left, to_left), (right, to_right), (own, mine)):
        upper = jnp.where(low_rows, term, zero)
        ref[part, :size] += upper
        ref[part, size:] += term - upper


def prepare_kernel(rows, cols, order, wave, probe, amp, wave_out, probe_out, amp_out, scales, peak):
    position = pl.program_id(0)
    row_at, col_at = rows[position], cols[position]
    parts = wave.shape[1]
    size = wave.shape[2]
    largest = None
    for part in range(parts):
        value = wave[0, part].astype(F32)
        folded = jnp.max(jnp.abs(value), axis=0, keepdims=True)
        largest = folded if largest is None else jnp.maximum(largest, folded)
        wave_out[0, part] = pltpu.roll(pltpu.roll(value, row_at, 0), col_at, 1).astype(BF16)
        value = probe[part * size : (part + 1) * size]
        probe_out[0, part] = pltpu.roll(pltpu.roll(value, row_at, 0), col_at, 1)
    amp_out[0] = dot(dot(order[0], amp[0]).astype(BF16), order[1]).astype(BF16)

    @pl.when(position == 0)
    def _():
        peak[...] = jnp.zeros_like(peak)

    peak[0:1] = jnp.maximum(peak[0:1], largest)

    @pl.when(position == pl.num_programs(0) - 1)
    def _():
        count = pl.num_programs(0) * (parts // 2)
        wave_peak = jnp.max(peak[0:1])
        probe_peak = jnp.max(jnp.abs(probe[...]))
        root = 2.0**0.5
        chi_bound = size * (2.0 * object_bound * wave_peak + amp_bound)
        second = count * root * wave_peak * chi_bound
        first = count * root * probe_peak * (root * object_bound * chi_bound)
        tile = lax.broadcasted_iota(jnp.int32, scales.shape, 0)
        scales[...] = jnp.maximum(jnp.where(tile < 4, second, first), 1e-30) * (1.0 / half_range)


def clear(refs):
    @pl.when(pl.program_id(0) == 0)
    def _():
        for ref in refs:
            ref[...] = jnp.zeros_like(ref)


def exit_kernel(rows, cols, tables, left_in, own_in, right_in, scales, wave, amp, back, left, own, right):
    position = pl.program_id(0)
    size = wave.shape[2]
    width = own_in.shape[2]
    half = size // 2
    count = wave.shape[1] // 2
    clear((left, own, right))
    low_rows, left_cols = masks(rows[position], cols[position], size, width)
    second_real = patch_of(left_in, own_in, right_in, 0, low_rows, left_cols)
    second_imag = patch_of(left_in, own_in, right_in, 1, low_rows, left_cols)
    fields = []
    for mode in range(count):
        mid_real, mid_imag = wave[0, mode].astype(F32), wave[0, count + mode].astype(F32)
        fields.append(
            (
                mid_real * second_real - mid_imag * second_imag,
                mid_real * second_imag + mid_imag * second_real,
            )
        )
    plus, minus = fold_rows(fields)
    plus, minus = fold_lanes(from_left(tables, 0, plus), from_left(tables, 1, minus), count)
    spectra = [from_right(plus, tables, 2), from_right(minus, tables, 3)]
    filtered = []
    for lane, spectrum in enumerate(spectra):
        rows_of = []
        for row in range(2):
            power = None
            for mode in range(count):
                block = spectrum[(2 * mode + row) * half : (2 * mode + row + 1) * half]
                squares = block[:, :half] * block[:, :half] + block[:, half:] * block[:, half:]
                power = squares if power is None else power + squares
            level = amp[0, row * half : (row + 1) * half, lane * half : (lane + 1) * half]
            factor = 1.0 - level.astype(F32) * jnp.minimum(lax.rsqrt(power), 1.0 / floor_level)
            rows_of.append(join([factor, factor], 1))
        filtered.append(spectrum * join(rows_of * count, 0))
    evens, odds = unfold_lanes(
        from_right(filtered[0], tables, 0), from_right(filtered[1], tables, 1), count
    )
    fields = unfold_rows(from_left(tables, 2, evens), from_left(tables, 3, odds), count)
    grad_real = grad_imag = None
    for mode, (chi_real, chi_imag) in enumerate(fields):
        mid_real, mid_imag = wave[0, mode].astype(F32), wave[0, count + mode].astype(F32)
        real = mid_real * chi_real + mid_imag * chi_imag
        imag = mid_real * chi_imag - mid_imag * chi_real
        grad_real = real if grad_real is None else grad_real + real
        grad_imag = imag if grad_imag is None else grad_imag + imag
        back[0, mode] = second_real * chi_real + second_imag * chi_imag
        back[0, count + mode] = second_real * chi_imag - second_imag * chi_real
    inverse = 1.0 / scales[0:1, :width]
    scatter(0, grad_real, inverse, left, own, right, low_rows, left_cols)
    scatter(1, grad_imag, inverse, left, own, right, low_rows, left_cols)


def back_kernel(rows, cols, tables, scales, back, probe, wave, left, own, right):
    position = pl.program_id(0)
    size = back.shape[2]
    width = own.shape[2]
    count = back.shape[1] // 2
    clear((left, own, right))
    low_rows, left_cols = masks(rows[position], cols[position], size, width)
    fields = [(back[0, mode], back[0, count + mode]) for mode in range(count)]
    plus, minus = fold_rows(fields)
    even, odd = from_left(tables, 0, plus), from_left(tables, 1, minus)
    plus, minus = fold_lanes(even + odd, even - odd, count)
    top, bottom = unfold_lanes(
        from_right(plus, tables, 2), from_right(minus, tables, 3), count
    )
    half = size // 2
    grad_real = grad_imag = None
    for mode in range(count):
        lanes = slice(mode * size, (mode + 1) * size)
        real = join([top[:half, lanes], bottom[:half, lanes]], 0)
        imag = join([top[half:, lanes], bottom[half:, lanes]], 0)
        wave[0, mode] = real
        wave[0, count + mode] = imag
        probe_real, probe_imag = probe[0, mode], probe[0, count + mode]
        term_real = probe_real * real + probe_imag * imag
        term_imag = probe_real * imag - probe_imag * real
        grad_real = term_real if grad_real is None else grad_real + term_real
        grad_imag = term_imag if grad_imag is None else grad_imag + term_imag
    inverse = 1.0 / scales[4:5, :width]
    scatter(0, grad_real, inverse, left, own, right, low_rows, left_cols)
    scatter(1, grad_imag, inverse, left, own, right, low_rows, left_cols)


def probe_kernel(rows, cols, left_in, own_in, right_in, wave, grad):
    position = pl.program_id(0)
    size = wave.shape[2]
    width = own_in.shape[2]
    count = wave.shape[1] // 2
    clear((grad,))
    row_at, col_at = rows[position], cols[position]
    low_rows, left_cols = masks(row_at, col_at, size, width)
    real = patch_of(left_in, own_in, right_in, 0, low_rows, left_cols)
    imag = patch_of(left_in, own_in, right_in, 1, low_rows, left_cols)
    row_back, col_back = size - row_at, size - col_at
    for mode in range(count):
        wave_real, wave_imag = wave[0, mode], wave[0, count + mode]
        for part, value in (
            (mode, real * wave_real + imag * wave_imag),
            (count + mode, real * wave_imag - imag * wave_real),
        ):
            value = pltpu.roll(pltpu.roll(value, row_back, 0), col_back, 1)
            grad[part * size : (part + 1) * size] += value


def shape_of(shape, kind=F32):
    return jax.ShapeDtypeStruct(shape, kind)


def block_of(shape):
    rest = (0,) * (len(shape) - 1)
    return pl.BlockSpec((1,) + tuple(shape[1:]), lambda p, *_: (p,) + rest)


def fixed(shape):
    zeros = (0,) * len(shape)
    return pl.BlockSpec(tuple(shape), lambda p, *_: zeros)


def call(kernel, count, ins, outs, scratch=(), flops=0, transcendentals=0):
    moved = sum(int(np.prod(a.shape)) * a.dtype.itemsize for a, _ in ins + outs)
    return pl.pallas_call(
        kernel,
        grid_spec=pltpu.PrefetchScalarGridSpec(
            num_scalar_prefetch=2,
            grid=(count,),
            in_specs=[block_of(a.shape) if cut else fixed(a.shape) for a, cut in ins[2:]],
            out_specs=[block_of(a.shape) if cut else fixed(a.shape) for a, cut in outs],
            scratch_shapes=list(scratch),
        ),
        out_shape=[a for a, _ in outs],
        cost_estimate=pl.CostEstimate(
            flops=flops, bytes_accessed=moved, transcendentals=transcendentals
        ),
        compiler_params=pltpu.CompilerParams(
            dimension_semantics=("arbitrary",), vmem_limit_bytes=48 * 1024 * 1024
        ),
    )(*[a for a, _ in ins])


def shifted(block, axis, distance):
    devices = range(lax.axis_size(axis))
    route = [(i - distance, i) for i in devices if i - distance in devices]
    return lax.ppermute(block, axis, route)


def swapped(block, axis, bit):
    return lax.ppermute(block, axis, [(i, i ^ bit) for i in range(lax.axis_size(axis))])


def halved_sum(block, dim, axis, bit, low):
    mine = (lax.axis_index(axis) // bit) % 2
    half = block.shape[dim] // 2
    pair = (half, 2) if low else (2, half)
    view = block.reshape(block.shape[:dim] + pair + block.shape[dim + 1 :])
    at = dim + 1 if low else dim
    keep = lax.dynamic_index_in_dim(view, mine, at, False)
    send = lax.dynamic_index_in_dim(view, 1 - mine, at, False)
    return keep + swapped(send, axis, bit)


def bits_of(axis):
    bit = lax.axis_size(axis) // 2
    bits = []
    while bit:
        bits.append(bit)
        bit //= 2
    return bits


def summed(values):
    axes = ("group", "tile")
    count = lax.axis_size("group") * lax.axis_size("tile")
    copies = jnp.broadcast_to(values[None], (count,) + values.shape)
    return jnp.sum(lax.all_to_all(copies, axes, 0, 0, tiled=True), axis=0)


def shards(object_slices, probe, mid_waves, amplitudes, row_offsets, col_offsets):
    row_count, strip_width = object_slices.shape[1:]
    size = probe.shape[1]
    count = mid_waves.shape[2]
    modes = probe.shape[0] // (2 * size)
    assert row_count == 2 * size and size == 2 * strip_width and size % 256 == 0
    groups, tiles = lax.axis_size("group"), lax.axis_size("tile")
    rows, cols = row_offsets.reshape(count), col_offsets.reshape(count)
    waves = mid_waves.reshape(count, 2 * modes, size, size)
    levels = amplitudes.reshape(count, size, size)
    first, second = object_slices[:2], object_slices[2:]
    left_second, right_second = shifted(second, "tile", 1), shifted(second, "tile", -1)
    left_first, right_first = shifted(first, "tile", 1), shifted(first, "tile", -1)

    planes = (count, 2 * modes, size, size)
    product = 2 * size**3
    rolled_waves, rolled_probe, ordered, scales = call(
        prepare_kernel,
        count,
        [
            (rows, 0),
            (cols, 0),
            (jnp.asarray(order_table(size)), 0),
            (waves, 1),
            (probe, 0),
            (levels, 1),
        ],
        [
            (shape_of(planes, BF16), 1),
            (shape_of(planes), 1),
            (shape_of(levels.shape, BF16), 1),
            (shape_of((8, strip_width)), 0),
        ],
        scratch=[pltpu.VMEM((8, size), F32)],
        flops=count * 2 * product,
    )
    left_scales, right_scales = shifted(scales, "tile", 1), shifted(scales, "tile", -1)
    rim = shape_of((2, row_count, strip_width))
    back, left_rim, own_second, right_rim = call(
        exit_kernel,
        count,
        [
            (rows, 0),
            (cols, 0),
            (jnp.asarray(dft_tables(size)), 0),
            (left_second, 0),
            (second, 0),
            (right_second, 0),
            (scales, 0),
            (rolled_waves, 1),
            (ordered, 1),
        ],
        [(shape_of(planes), 1), (rim, 0), (rim, 0), (rim, 0)],
        flops=count * modes * 24 * product,
    )
    from_right_second = shifted(left_rim.astype(jnp.float16), "tile", -1)
    from_left_second = shifted(right_rim.astype(jnp.float16), "tile", 1)
    waves_back, left_rim, own_first, right_rim = call(
        back_kernel,
        count,
        [
            (rows, 0),
            (cols, 0),
            (jnp.asarray(back_tables(size)), 0),
            (scales, 0),
            (back, 1),
            (rolled_probe, 1),
        ],
        [(shape_of(planes), 1), (rim, 0), (rim, 0), (rim, 0)],
        flops=count * modes * 12 * product,
    )
    from_right_first = shifted(left_rim.astype(jnp.float16), "tile", -1)
    from_left_first = shifted(right_rim.astype(jnp.float16), "tile", 1)
    (grad_probe,) = call(
        probe_kernel,
        count,
        [
            (rows, 0),
            (cols, 0),
            (left_first, 0),
            (first, 0),
            (right_first, 0),
            (waves_back, 1),
        ],
        [(shape_of(probe.shape), 0)],
        flops=count * 8 * modes * size * size,
    )

    share = probe.shape[0] // tiles
    piece = share // groups
    part = grad_probe.reshape(tiles, groups, piece, size)
    for bit in reversed(bits_of("group")):
        part = halved_sum(part, 1, "group", bit, True)
    for bit in bits_of("tile"):
        part = halved_sum(part, 0, "tile", bit, False)
    part = part.reshape(piece, size)
    probe_squares = jnp.sum(part * part)

    own_second = (
        own_second
        + from_right_second.astype(F32) * right_scales[0, 0]
        + from_left_second.astype(F32) * left_scales[0, 0]
    )
    own_first = (
        own_first
        + from_right_first.astype(F32) * right_scales[4, 0]
        + from_left_first.astype(F32) * left_scales[4, 0]
    )
    own_grad = jnp.concatenate([own_first, own_second])
    object_squares = jnp.sum(own_grad * own_grad)
    object_total = summed(object_squares.reshape(1))[0]
    probe_total = summed(probe_squares.reshape(1))[0]
    object_count = 4 * row_count * strip_width * groups * tiles
    object_rms = jnp.sqrt(object_total / object_count + epsilon)
    object_new = object_slices.astype(F32) - object_step * own_grad / object_rms

    whole = part
    for bit in reversed(bits_of("group")):
        other = swapped(whole, "group", bit)
        mine = (lax.axis_index("group") // bit) % 2
        whole = jnp.where(
            mine == 0,
            jnp.concatenate([whole, other]),
            jnp.concatenate([other, whole]),
        )
    probe_rms = jnp.sqrt(probe_total / probe.size + epsilon)
    start_row = lax.axis_index("tile") * share
    probe_rows = lax.dynamic_slice_in_dim(probe, start_row, share, 0)
    probe_new = probe_rows - probe_step * whole / probe_rms
    return (object_new, probe_new)


def solution(mesh):
    return jax.shard_map(
        shards,
        mesh=mesh,
        in_specs=(
            P(None, "group", "tile"),
            P(),
            P("group", "tile", None, None, None, None, None),
            P("group", "tile", None, None, None),
            P("group", "tile", None),
            P("group", "tile", None),
        ),
        out_specs=(P(None, "group", "tile"), P("tile", None)),
        check_vma=False,
    )
```

profile of v0, /device:TPU:0, one launch (start us, length us, event | category | flops | bytes accessed | tf_op | source)
XLA Modules:
  0.0 137.0 jit_solution(4782331582450450173)
XLA Ops:
  0.6 1.1 fusion.3
  1.7 4.9 %collective-permute-start = (bf16[2,512,128]{2,1,0:T(8,128)(2,1)S(1)}, bf16[2,512,128]{2,1,0:T(8,128)(2,1)S(1)}, u32[]{:S(2)}, u32[]{:S(2)}) collective-permute-start(bf16[2,512,128]{2,1,0:T(8,128)(2,1)S(1)} %get-tuple-element.29.own_in), channel_id=1, source_target_pairs={{0,1},{1,2},{2,3},{3,4},{4,5},{5,6},{6,7},{8,9},{9,10},{10,11},{11... | collective-permute-start | bytes 786440 | tf_op jit(solution)/shard_map/ppermute | solution.py:361
  6.6 1.3 collective-permute-start.1
  7.9 4.6 %collective-permute-start.8 = (bf16[2,512,128]{2,1,0:T(8,128)(2,1)S(1)}, bf16[2,512,128]{2,1,0:T(8,128)(2,1)S(1)}, u32[]{:S(2)}, u32[]{:S(2)}) collective-permute-start(bf16[2,512,128]{2,1,0:T(8,128)(2,1)S(1)} %get-tuple-element.28.own_in), channel_id=1, source_target_pairs={{0,1},{1,2},{2,3},{3,4},{4,5},{5,6},{6,7},{8,9},{9,10},{10,11},{11... | collective-permute-start | bytes 786440 | tf_op jit(solution)/shard_map/ppermute | solution.py:361
  12.5 1.3 collective-permute-start.9
  13.8 1.4 %copy-done = bf16[1,1,3,2,2,256,256]{6,5,4,3,2,1,0:T(8,128)(2,1)S(1)} copy-done((bf16[1,1,3,2,2,256,256]{6,5,4,3,2,1,0:T(8,128)(2,1)S(1)}, bf16[1,1,3,2,2,256,256]{6,5,4,3,2,1,0:T(8,128)(2,1)}, u32[]{:S(2)}) %copy-start) | copy-done | bytes 1572888
  15.2 1.2 copy-done.1
  16.5 1.0 copy-done.6
  17.4 0.9 copy-done.7
  19.7 4.5 %shard_map.104 = (bf16[3,4,256,256]{3,2,1,0:T(8,128)(2,1)S(1)}, f32[3,4,256,256]{3,2,1,0:T(8,128)}, bf16[3,256,256]{2,1,0:T(8,128)(2,1)S(1)}, f32[8,128]{1,0:T(8,128)S(1)}) custom-call(s32[3]{0:T(128)S(1)} %bitcast.30, s32[3]{0:T(128)S(1)} %bitcast.34, bf16[2,256,256]{2,1,0:T(8,128)(2,1)S(1)} %copy-done.7, bf16[3,4,256,256]{3,2,1,0:T(8,128)(2,1)S(1)} %bitcast.28, ...), custom_call_target="tpu_custom_call" | custom-call | flops 201326592 | bytes 8392728 | tf_op jit(solution)/shard_map/pallas_call | solution.py:339
  24.5 10.5 %shard_map.105 = (f32[3,4,256,256]{3,2,1,0:T(8,128)}, f32[2,512,128]{2,1,0:T(8,128)S(1)}, f32[2,512,128]{2,1,0:T(8,128)S(1)}, f32[2,512,128]{2,1,0:T(8,128)S(1)}) custom-call(s32[3]{0:T(128)S(1)} %bitcast.31, s32[3]{0:T(128)S(1)} %bitcast.35, bf16[4,2,256,256]{3,2,1,0:T(8,128)(2,1)S(1)} %copy-done.15, bf16[2,512,128]{2,1,0:T(8,128)(2,1)S(1)} %collective-permute-done.left_in, ...), custom_call_target="tpu_custom_call" | custom-call | flops 4831838208 | bytes 8523800 | tf_op jit(solution)/shard_map/pallas_call | solution.py:339
  35.0 0.8 copy-done.4
  35.8 6.7 %shard_map.106 = (f32[3,4,256,256]{3,2,1,0:T(8,128)S(1)}, f32[2,512,128]{2,1,0:T(8,128)S(1)}, f32[2,512,128]{2,1,0:T(8,128)S(1)}, f32[2,512,128]{2,1,0:T(8,128)S(1)}) custom-call(s32[3]{0:T(128)S(1)} %bitcast.32, s32[3]{0:T(128)S(1)} %bitcast.36, bf16[4,2,256,256]{3,2,1,0:T(8,128)(2,1)S(1)} %copy-done.14, f32[8,128]{1,0:T(8,128)S(1)} %get-tuple-element.14.scales, ...), custom_call_target="tpu_custom_call" | custom-call | flops 2415919104 | bytes 12062744 | tf_op jit(solution)/shard_map/pallas_call | solution.py:339
  42.5 0.7 copy-done.8
  44.0 0.9 copy-done.9
  44.9 0.9 copy-done.11
  45.9 4.1 %shard_map.107 = f32[1024,256]{1,0:T(8,128)S(1)} custom-call(s32[3]{0:T(128)S(1)} %bitcast.33, s32[3]{0:T(128)S(1)} %bitcast.37, bf16[2,512,128]{2,1,0:T(8,128)(2,1)S(1)} %copy-done.9, bf16[2,512,128]{2,1,0:T(8,128)(2,1)S(1)} %get-tuple-element.28.own_in, bf16[2,512,128]{2,1,0:T(8,128)(2,1)S(1)} %copy-done.11, f32[3,4,256,256]{3,2,1,0:T(8,128)S(1)} %get-tuple-element.25.wave), custom_call_target="tpu_custom_call" | custom-call | flops 3145728 | bytes 4980760 | tf_op jit(solution)/shard_map/pallas_call | solution.py:339
  50.0 0.8 dynamic-slice_bitcast_fusion
  50.9 2.2 %collective-permute-done.10 = f32[8,2,32,256]{3,2,1,0:T(8,128)} collective-permute-done((f32[8,2,32,256]{3,2,1,0:T(8,128)}, f32[8,2,32,256]{3,2,1,0:T(8,128)}, u32[]{:S(2)}, u32[]{:S(2)}) %collective-permute-start.10) | collective-permute-done | bytes 524320 | tf_op jit(solution)/shard_map/ppermute | solution.py:365
  53.1 1.1 bitcast_add_fusion
  54.3 0.8 copy-done.16
  55.1 1.6 %collective-permute-start.11 = (f32[8,1,32,256]{3,2,1,0:T(8,128)S(1)}, f32[8,1,32,256]{3,2,1,0:T(8,128)S(1)}, u32[]{:S(2)}, u32[]{:S(2)}) collective-permute-start(f32[8,1,32,256]{3,2,1,0:T(8,128)S(1)} %constant_dynamic-slice_fusion.1), channel_id=1, source_target_pairs={{0,16},{8,24},{16,0},{24,8},{1,17},{9,25},{17,1},{25,9},{2,18},{10... | collective-permute-start | bytes 786440 | tf_op jit(solution)/shard_map/ppermute | solution.py:365
  56.6 6.8 %collective-permute-done.11 = f32[8,1,32,256]{3,2,1,0:T(8,128)S(1)} collective-permute-done((f32[8,1,32,256]{3,2,1,0:T(8,128)S(1)}, f32[8,1,32,256]{3,2,1,0:T(8,128)S(1)}, u32[]{:S(2)}, u32[]{:S(2)}) %collective-permute-start.11) | collective-permute-done | bytes 262176 | tf_op jit(solution)/shard_map/ppermute | solution.py:365
  63.5 1.0 dynamic-slice_add_fusion
  65.2 5.2 %collective-permute-start.12 = (f32[4,1,32,256]{3,2,0,1:T(8,128)}, f32[4,1,32,256]{3,2,0,1:T(8,128)S(1)}, u32[]{:S(2)}, u32[]{:S(2)}) collective-permute-start(f32[4,1,32,256]{3,2,0,1:T(8,128)} %dynamic-slice_bitcast_fusion.1), channel_id=1, source_target_pairs={{0,4},{1,5},{2,6},{3,7},{4,0},{5,1},{6,2},{7,3},{8,12},{9,13},{10,... | collective-permute-start | bytes 393224 | tf_op jit(solution)/shard_map/ppermute | solution.py:365
  70.4 2.0 %collective-permute-start.5 = (f32[8,128]{1,0:T(8,128)S(1)}, f32[8,128]{1,0:T(8,128)S(1)}, u32[]{:S(2)}, u32[]{:S(2)}) collective-permute-start(f32[8,128]{1,0:T(8,128)S(1)} %get-tuple-element.14.scales), channel_id=1, source_target_pairs={{0,1},{1,2},{2,3},{3,4},{4,5},{5,6},{6,7},{8,9},{9,10},{10,11},{11... | collective-permute-start | bytes 12296 | tf_op jit(solution)/shard_map/ppermute | solution.py:361
  72.4 1.3 collective-permute-start.3
  74.4 2.0 %collective-permute-done.12 = f32[4,1,32,256]{3,2,0,1:T(8,128)S(1)} collective-permute-done((f32[4,1,32,256]{3,2,0,1:T(8,128)}, f32[4,1,32,256]{3,2,0,1:T(8,128)S(1)}, u32[]{:S(2)}, u32[]{:S(2)}) %collective-permute-start.12) | collective-permute-done | bytes 131104 | tf_op jit(solution)/shard_map/ppermute | solution.py:365
  76.4 3.1 %collective-permute-start.13 = (f32[2,1,32,256]{3,2,1,0:T(8,128)S(1)}, f32[2,1,32,256]{3,2,1,0:T(8,128)S(1)}, u32[]{:S(2)}, u32[]{:S(2)}) collective-permute-start(f32[2,1,32,256]{3,2,1,0:T(8,128)S(1)} %dynamic-slice_bitcast_fusion.2), channel_id=1, source_target_pairs={{0,2},{1,3},{2,0},{3,1},{4,6},{5,7},{6,4},{7,5},{8,10},{9,11},{10,... | collective-permute-start | bytes 196616 | tf_op jit(solution)/shard_map/ppermute | solution.py:365
  80.1 4.2 %collective-permute-start.7 = (f16[2,512,128]{2,1,0:T(8,128)(2,1)S(1)}, f16[2,512,128]{2,1,0:T(8,128)(2,1)S(1)}, u32[]{:S(2)}, u32[]{:S(2)}) collective-permute-start(f16[2,512,128]{2,1,0:T(8,128)(2,1)S(1)} %convert_element_type.34), channel_id=1, source_target_pairs={{0,1},{1,2},{2,3},{3,4},{4,5},{5,6},{6,7},{8,9},{9,10},{10,11},{11... | collective-permute-start | bytes 786440 | tf_op jit(solution)/shard_map/ppermute | solution.py:361
  84.4 1.3 collective-permute-start.6
  85.7 4.7 %collective-permute-start.4 = (f16[2,512,128]{2,1,0:T(8,128)(2,1)S(1)}, f16[2,512,128]{2,1,0:T(8,128)(2,1)S(1)}, u32[]{:S(2)}, u32[]{:S(2)}) collective-permute-start(f16[2,512,128]{2,1,0:T(8,128)(2,1)S(1)} %convert_element_type.30), channel_id=1, source_target_pairs={{0,1},{1,2},{2,3},{3,4},{4,5},{5,6},{6,7},{8,9},{9,10},{10,11},{11... | collective-permute-start | bytes 786440 | tf_op jit(solution)/shard_map/ppermute | solution.py:361
  90.5 1.3 collective-permute-start.2
  91.8 2.7 %collective-permute-start.14 = (f32[1,1,32,256]{3,2,1,0:T(8,128)S(1)}, f32[1,1,32,256]{3,2,1,0:T(8,128)S(1)}, u32[]{:S(2)}, u32[]{:S(2)}) collective-permute-start(f32[1,1,32,256]{3,2,1,0:T(8,128)S(1)} %constant_dynamic-slice_fusion), channel_id=1, source_target_pairs={{0,1},{1,0},{2,3},{3,2},{4,5},{5,4},{6,7},{7,6},{8,9},{9,8},{10,11... | collective-permute-start | bytes 98312 | tf_op jit(solution)/shard_map/ppermute | solution.py:365
  94.5 7.1 %collective-permute-done.7 = f16[2,512,128]{2,1,0:T(8,128)(2,1)S(1)} collective-permute-done((f16[2,512,128]{2,1,0:T(8,128)(2,1)S(1)}, f16[2,512,128]{2,1,0:T(8,128)(2,1)S(1)}, u32[]{:S(2)}, u32[]{:S(2)}) %collective-permute-start.7) | collective-permute-done | bytes 262176 | tf_op jit(solution)/shard_map/ppermute | solution.py:361
  101.6 1.4 %multiply_add_fusion = f32[2,512,128]{2,1,0:T(8,128)S(1)} fusion(f16[2,512,128]{2,1,0:T(8,128)(2,1)S(1)} %collective-permute-done.7, f32[2,512,128]{2,1,0:T(8,128)S(1)} %copy-done.5, f16[2,512,128]{2,1,0:T(8,128)(2,1)S(1)} %collective-permute-done.6, f32[]{:T(128)} %bitcast.7, f32[]{:T(128)} %bitcast.6), kind=kLoop, calls=%fused_computation.5 | loop fusion | flops 786432 | bytes 1572872 | tf_op jit(solution)/shard_map/add | solution.py:494
  103.0 2.2 %collective-permute-done.14 = f32[1,1,32,256]{3,2,1,0:T(8,128)S(1)} collective-permute-done((f32[1,1,32,256]{3,2,1,0:T(8,128)S(1)}, f32[1,1,32,256]{3,2,1,0:T(8,128)S(1)}, u32[]{:S(2)}, u32[]{:S(2)}) %collective-permute-start.14) | collective-permute-done | bytes 32800 | tf_op jit(solution)/shard_map/ppermute | solution.py:365
  105.8 1.4 %multiply_add_fusion.1 = f32[2,512,128]{2,1,0:T(8,128)S(1)} fusion(f16[2,512,128]{2,1,0:T(8,128)(2,1)S(1)} %collective-permute-done.4, f32[2,512,128]{2,1,0:T(8,128)S(1)} %copy-done.3, f16[2,512,128]{2,1,0:T(8,128)(2,1)S(1)} %collective-permute-done.2, f32[]{:T(128)} %bitcast.5, f32[]{:T(128)} %bitcast.4), kind=kLoop, calls=%fused_computation.6 | loop fusion | flops 786432 | bytes 1572872 | tf_op jit(solution)/shard_map/add | solution.py:499
  107.2 0.9 multiply_reduce_fusion
  108.1 1.3 broadcast_in_dim.4
  109.3 5.5 %all-to-all-start = ((f32[32,1,1]{2,1,0:T(1,128)}), f32[32,1,1]{2,1,0:T(1,128)S(1)}, u32[]{:S(2)}, u32[]{:S(2)}) async-start(f32[32,1,1]{2,1,0:T(1,128)} %broadcast_in_dim.4), calls=%async_computation | async-start | bytes 32768 | tf_op jit(solution)/shard_map/all_to_all | solution.py:392
  114.9 7.1 %all-to-all-done = f32[32,1,1]{2,1,0:T(1,128)S(1)} async-done(((f32[32,1,1]{2,1,0:T(1,128)}), f32[32,1,1]{2,1,0:T(1,128)S(1)}, u32[]{:S(2)}, u32[]{:S(2)}) %all-to-all-start) | async-done | bytes 160 | tf_op jit(solution)/shard_map/all_to_all | solution.py:392
  123.3 1.2 broadcast_in_dim.5
  124.4 2.5 %all-to-all-start.1 = ((f32[32,1,1]{2,1,0:T(1,128)}), f32[32,1,1]{2,1,0:T(1,128)S(1)}, u32[]{:S(2)}, u32[]{:S(2)}) async-start(f32[32,1,1]{2,1,0:T(1,128)} %broadcast_in_dim.5), calls=%async_computation.1 | async-start | bytes 32768 | tf_op jit(solution)/shard_map/all_to_all | solution.py:392
  127.0 1.7 %collective-permute-start.16 = (f32[64,256]{1,0:T(8,128)S(1)}, f32[64,256]{1,0:T(8,128)S(1)}, u32[]{:S(2)}, u32[]{:S(2)}) collective-permute-start(f32[64,256]{1,0:T(8,128)S(1)} %maximum_select_fusion.1), channel_id=1, source_target_pairs={{0,16},{8,24},{16,0},{24,8},{1,17},{9,25},{17,1},{25,9},{2,18},{10... | collective-permute-start | bytes 196616 | tf_op jit(solution)/shard_map/ppermute | solution.py:365
  128.7 1.1 divide_subtract_fusion
  129.8 4.2 %all-to-all-done.1 = f32[32,1,1]{2,1,0:T(1,128)S(1)} async-done(((f32[32,1,1]{2,1,0:T(1,128)}), f32[32,1,1]{2,1,0:T(1,128)S(1)}, u32[]{:S(2)}, u32[]{:S(2)}) %all-to-all-start.1) | async-done | bytes 160 | tf_op jit(solution)/shard_map/all_to_all | solution.py:392
  135.4 1.6 %fusion.2 = f32[128,256]{1,0:T(8,128)} fusion(f32[64,256]{1,0:T(8,128)S(1)} %collective-permute-done.16, f32[64,256]{1,0:T(8,128)S(1)} %maximum_select_fusion.1, f32[1024,256]{1,0:T(8,128)} %probe.1, s32[]{:T(128)S(6)} %select_n.95, f32[]{:T(128)S(6)} %sqrt.7, pred[]{:T(512)S(6)} %eq.14), kind=kLoop, calls=%fused_computation.11 | loop fusion | flops 196608 | bytes 393225 | tf_op jit(solution)/shard_map/sub | solution.py:523
  (57 shorter events, 6.3 us)
Async XLA Ops:
  1.7 22.8 %collective-permute-start = (bf16[2,512,128]{2,1,0:T(8,128)(2,1)S(1)}, bf16[2,512,128]{2,1,0:T(8,128)(2,1)S(1)}, u32[]{:S(2)}, u32[]{:S(2)}) collective-permute-start(bf16[2,512,128]{2,1,0:T(8,128)(2,1)S(1)} %get-tuple-element.29.own_in), channel_id=1, source_target_pairs={{0,1},{1,2},{2,3},{3,4},{4,5},{5,6},{6,7},{8,9},{9,10},{10,11},{11... | collective-permute-start | bytes 786440 | tf_op jit(solution)/shard_map/ppermute | solution.py:361
  6.6 17.9 %collective-permute-start.1 = (bf16[2,512,128]{2,1,0:T(8,128)(2,1)S(1)}, bf16[2,512,128]{2,1,0:T(8,128)(2,1)S(1)}, u32[]{:S(2)}, u32[]{:S(2)}) collective-permute-start(bf16[2,512,128]{2,1,0:T(8,128)(2,1)S(1)} %get-tuple-element.29.own_in), channel_id=1, source_target_pairs={{1,0},{2,1},{3,2},{4,3},{5,4},{6,5},{7,6},{9,8},{10,9},{11,10},{12... | collective-permute-start | bytes 786440 | tf_op jit(solution)/shard_map/ppermute | solution.py:361
  7.9 34.6 %collective-permute-start.8 = (bf16[2,512,128]{2,1,0:T(8,128)(2,1)S(1)}, bf16[2,512,128]{2,1,0:T(8,128)(2,1)S(1)}, u32[]{:S(2)}, u32[]{:S(2)}) collective-permute-start(bf16[2,512,128]{2,1,0:T(8,128)(2,1)S(1)} %get-tuple-element.28.own_in), channel_id=1, source_target_pairs={{0,1},{1,2},{2,3},{3,4},{4,5},{5,6},{6,7},{8,9},{9,10},{10,11},{11... | collective-permute-start | bytes 786440 | tf_op jit(solution)/shard_map/ppermute | solution.py:361
  12.5 30.8 %collective-permute-start.9 = (bf16[2,512,128]{2,1,0:T(8,128)(2,1)S(1)}, bf16[2,512,128]{2,1,0:T(8,128)(2,1)S(1)}, u32[]{:S(2)}, u32[]{:S(2)}) collective-permute-start(bf16[2,512,128]{2,1,0:T(8,128)(2,1)S(1)} %get-tuple-element.28.own_in), channel_id=1, source_target_pairs={{1,0},{2,1},{3,2},{4,3},{5,4},{6,5},{7,6},{9,8},{10,9},{11,10},{12... | collective-permute-start | bytes 786440 | tf_op jit(solution)/shard_map/ppermute | solution.py:361
  13.8 1.4 %copy-start = (bf16[1,1,3,2,2,256,256]{6,5,4,3,2,1,0:T(8,128)(2,1)S(1)}, bf16[1,1,3,2,2,256,256]{6,5,4,3,2,1,0:T(8,128)(2,1)}, u32[]{:S(2)}) copy-start(bf16[1,1,3,2,2,256,256]{6,5,4,3,2,1,0:T(8,128)(2,1)} %param.11) | copy-start | bytes 4718596
  15.2 1.2 copy-start.1
  16.4 1.0 copy-start.6
  17.4 0.9 copy-start.7
  18.4 0.7 copy-start.12
  19.1 0.7 copy-start.13
  19.7 4.8 %copy-start.15 = (bf16[4,2,256,256]{3,2,1,0:T(8,128)(2,1)S(1)}, bf16[4,2,256,256]{3,2,1,0:T(8,128)(2,1)}, u32[]{:S(2)}) copy-start(bf16[4,2,256,256]{3,2,1,0:T(8,128)(2,1)} %constant.149.clone.tables) | copy-start | bytes 3145732
  24.5 11.3 %copy-start.14 = (bf16[4,2,256,256]{3,2,1,0:T(8,128)(2,1)S(1)}, bf16[4,2,256,256]{3,2,1,0:T(8,128)(2,1)}, u32[]{:S(2)}) copy-start(bf16[4,2,256,256]{3,2,1,0:T(8,128)(2,1)} %constant.150.clone.tables) | copy-start | bytes 3145732
  35.0 0.8 copy-start.4
  42.5 7.5 %copy-start.2 = (f32[2,512,128]{2,1,0:T(8,128)}, f32[2,512,128]{2,1,0:T(8,128)S(1)}, u32[]{:S(2)}) copy-start(f32[2,512,128]{2,1,0:T(8,128)S(1)} %get-tuple-element.19) | copy-start | bytes 1572868
  42.5 0.7 copy-start.8
  43.3 0.7 copy-start.10
  44.0 0.9 copy-start.9
  44.9 0.9 copy-start.11
  50.9 2.3 %collective-permute-start.10 = (f32[8,2,32,256]{3,2,1,0:T(8,128)}, f32[8,2,32,256]{3,2,1,0:T(8,128)}, u32[]{:S(2)}, u32[]{:S(2)}) collective-permute-start(f32[8,2,32,256]{3,2,1,0:T(8,128)} %dynamic-slice_bitcast_fusion), channel_id=1, source_target_pairs={{0,8},{8,0},{16,24},{24,16},{1,9},{9,1},{17,25},{25,17},{2,10},{10... | collective-permute-start | bytes 1572872 | tf_op jit(solution)/shard_map/ppermute | solution.py:365
  54.3 0.8 copy-start.16
  55.1 46.5 %copy-start.5 = (f32[2,512,128]{2,1,0:T(8,128)S(1)}, f32[2,512,128]{2,1,0:T(8,128)}, u32[]{:S(2)}) copy-start(f32[2,512,128]{2,1,0:T(8,128)} %copy-done.4) | copy-start | bytes 1572868
  55.1 8.4 %collective-permute-start.11 = (f32[8,1,32,256]{3,2,1,0:T(8,128)S(1)}, f32[8,1,32,256]{3,2,1,0:T(8,128)S(1)}, u32[]{:S(2)}, u32[]{:S(2)}) collective-permute-start(f32[8,1,32,256]{3,2,1,0:T(8,128)S(1)} %constant_dynamic-slice_fusion.1), channel_id=1, source_target_pairs={{0,16},{8,24},{16,0},{24,8},{1,17},{9,25},{17,1},{25,9},{2,18},{10... | collective-permute-start | bytes 786440 | tf_op jit(solution)/shard_map/ppermute | solution.py:365
  64.5 41.3 %copy-start.3 = (f32[2,512,128]{2,1,0:T(8,128)S(1)}, f32[2,512,128]{2,1,0:T(8,128)}, u32[]{:S(2)}) copy-start(f32[2,512,128]{2,1,0:T(8,128)} %copy-done.2) | copy-start | bytes 1572868
  65.2 11.2 %collective-permute-start.12 = (f32[4,1,32,256]{3,2,0,1:T(8,128)}, f32[4,1,32,256]{3,2,0,1:T(8,128)S(1)}, u32[]{:S(2)}, u32[]{:S(2)}) collective-permute-start(f32[4,1,32,256]{3,2,0,1:T(8,128)} %dynamic-slice_bitcast_fusion.1), channel_id=1, source_target_pairs={{0,4},{1,5},{2,6},{3,7},{4,0},{5,1},{6,2},{7,3},{8,12},{9,13},{10,... | collective-permute-start | bytes 393224 | tf_op jit(solution)/shard_map/ppermute | solution.py:365
  70.4 3.4 %collective-permute-start.5 = (f32[8,128]{1,0:T(8,128)S(1)}, f32[8,128]{1,0:T(8,128)S(1)}, u32[]{:S(2)}, u32[]{:S(2)}) collective-permute-start(f32[8,128]{1,0:T(8,128)S(1)} %get-tuple-element.14.scales), channel_id=1, source_target_pairs={{0,1},{1,2},{2,3},{3,4},{4,5},{5,6},{6,7},{8,9},{9,10},{10,11},{11... | collective-permute-start | bytes 12296 | tf_op jit(solution)/shard_map/ppermute | solution.py:361
  72.4 7.1 %collective-permute-start.3 = (f32[8,128]{1,0:T(8,128)S(1)}, f32[8,128]{1,0:T(8,128)S(1)}, u32[]{:S(2)}, u32[]{:S(2)}) collective-permute-start(f32[8,128]{1,0:T(8,128)S(1)} %get-tuple-element.14.scales), channel_id=1, source_target_pairs={{1,0},{2,1},{3,2},{4,3},{5,4},{6,5},{7,6},{9,8},{10,9},{11,10},{12... | collective-permute-start | bytes 12296 | tf_op jit(solution)/shard_map/ppermute | solution.py:361
  76.4 15.4 %collective-permute-start.13 = (f32[2,1,32,256]{3,2,1,0:T(8,128)S(1)}, f32[2,1,32,256]{3,2,1,0:T(8,128)S(1)}, u32[]{:S(2)}, u32[]{:S(2)}) collective-permute-start(f32[2,1,32,256]{3,2,1,0:T(8,128)S(1)} %dynamic-slice_bitcast_fusion.2), channel_id=1, source_target_pairs={{0,2},{1,3},{2,0},{3,1},{4,6},{5,7},{6,4},{7,5},{8,10},{9,11},{10,... | collective-permute-start | bytes 196616 | tf_op jit(solution)/shard_map/ppermute | solution.py:365
  80.1 21.4 %collective-permute-start.7 = (f16[2,512,128]{2,1,0:T(8,128)(2,1)S(1)}, f16[2,512,128]{2,1,0:T(8,128)(2,1)S(1)}, u32[]{:S(2)}, u32[]{:S(2)}) collective-permute-start(f16[2,512,128]{2,1,0:T(8,128)(2,1)S(1)} %convert_element_type.34), channel_id=1, source_target_pairs={{0,1},{1,2},{2,3},{3,4},{4,5},{5,6},{6,7},{8,9},{9,10},{10,11},{11... | collective-permute-start | bytes 786440 | tf_op jit(solution)/shard_map/ppermute | solution.py:361
  84.4 17.2 %collective-permute-start.6 = (f16[2,512,128]{2,1,0:T(8,128)(2,1)S(1)}, f16[2,512,128]{2,1,0:T(8,128)(2,1)S(1)}, u32[]{:S(2)}, u32[]{:S(2)}) collective-permute-start(f16[2,512,128]{2,1,0:T(8,128)(2,1)S(1)} %convert_element_type.32), channel_id=1, source_target_pairs={{1,0},{2,1},{3,2},{4,3},{5,4},{6,5},{7,6},{9,8},{10,9},{11,10},{12... | collective-permute-start | bytes 786440 | tf_op jit(solution)/shard_map/ppermute | solution.py:361
  85.7 43.1 %copy-start.17 = (bf16[4,512,128]{2,1,0:T(8,128)(2,1)S(1)}, bf16[4,512,128]{2,1,0:T(8,128)(2,1)}, u32[]{:S(2)}) copy-start(bf16[4,512,128]{2,1,0:T(8,128)(2,1)} %param.9) | copy-start | bytes 1572868
  85.7 20.1 %collective-permute-start.4 = (f16[2,512,128]{2,1,0:T(8,128)(2,1)S(1)}, f16[2,512,128]{2,1,0:T(8,128)(2,1)S(1)}, u32[]{:S(2)}, u32[]{:S(2)}) collective-permute-start(f16[2,512,128]{2,1,0:T(8,128)(2,1)S(1)} %convert_element_type.30), channel_id=1, source_target_pairs={{0,1},{1,2},{2,3},{3,4},{4,5},{5,6},{6,7},{8,9},{9,10},{10,11},{11... | collective-permute-start | bytes 786440 | tf_op jit(solution)/shard_map/ppermute | solution.py:361
  90.5 15.3 %collective-permute-start.2 = (f16[2,512,128]{2,1,0:T(8,128)(2,1)S(1)}, f16[2,512,128]{2,1,0:T(8,128)(2,1)S(1)}, u32[]{:S(2)}, u32[]{:S(2)}) collective-permute-start(f16[2,512,128]{2,1,0:T(8,128)(2,1)S(1)} %convert_element_type.28), channel_id=1, source_target_pairs={{1,0},{2,1},{3,2},{4,3},{5,4},{6,5},{7,6},{9,8},{10,9},{11,10},{12... | collective-permute-start | bytes 786440 | tf_op jit(solution)/shard_map/ppermute | solution.py:361
  91.8 13.4 %collective-permute-start.14 = (f32[1,1,32,256]{3,2,1,0:T(8,128)S(1)}, f32[1,1,32,256]{3,2,1,0:T(8,128)S(1)}, u32[]{:S(2)}, u32[]{:S(2)}) collective-permute-start(f32[1,1,32,256]{3,2,1,0:T(8,128)S(1)} %constant_dynamic-slice_fusion), channel_id=1, source_target_pairs={{0,1},{1,0},{2,3},{3,2},{4,5},{5,4},{6,7},{7,6},{8,9},{9,8},{10,11... | collective-permute-start | bytes 98312 | tf_op jit(solution)/shard_map/ppermute | solution.py:365
  105.8 21.2 %collective-permute-start.15 = (f32[32,256]{1,0:T(8,128)S(1)}, f32[32,256]{1,0:T(8,128)S(1)}, u32[]{:S(2)}, u32[]{:S(2)}) collective-permute-start(f32[32,256]{1,0:T(8,128)S(1)} %get-tuple-element.27), channel_id=1, source_target_pairs={{0,8},{8,0},{16,24},{24,16},{1,9},{9,1},{17,25},{25,17},{2,10},{10... | collective-permute-start | bytes 98312 | tf_op jit(solution)/shard_map/ppermute | solution.py:365
  109.3 12.6 %all-to-all-start = ((f32[32,1,1]{2,1,0:T(1,128)}), f32[32,1,1]{2,1,0:T(1,128)S(1)}, u32[]{:S(2)}, u32[]{:S(2)}) async-start(f32[32,1,1]{2,1,0:T(1,128)} %broadcast_in_dim.4), calls=%async_computation | async-start | bytes 32768 | tf_op jit(solution)/shard_map/all_to_all | solution.py:392
  124.4 9.6 %all-to-all-start.1 = ((f32[32,1,1]{2,1,0:T(1,128)}), f32[32,1,1]{2,1,0:T(1,128)S(1)}, u32[]{:S(2)}, u32[]{:S(2)}) async-start(f32[32,1,1]{2,1,0:T(1,128)} %broadcast_in_dim.5), calls=%async_computation.1 | async-start | bytes 32768 | tf_op jit(solution)/shard_map/all_to_all | solution.py:392
  127.0 8.4 %collective-permute-start.16 = (f32[64,256]{1,0:T(8,128)S(1)}, f32[64,256]{1,0:T(8,128)S(1)}, u32[]{:S(2)}, u32[]{:S(2)}) collective-permute-start(f32[64,256]{1,0:T(8,128)S(1)} %maximum_select_fusion.1), channel_id=1, source_target_pairs={{0,16},{8,24},{16,0},{24,8},{1,17},{9,25},{17,1},{25,9},{2,18},{10... | collective-permute-start | bytes 196616 | tf_op jit(solution)/shard_map/ppermute | solution.py:365
where the time goes:
time: 138 us; the launch traced here: 137 us
  starting transfers between devices  49.2 us (36%)
  waiting for transfers between devices  31.9 us (23%)
  Pallas kernels  25.8 us (19%)
  local copies, waits for them, and re-layouts  17.1 us (12%)
  other arithmetic  10.5 us (8%)
  between operations  2.43 us (2%)
    ppermute x10, starting transfers between devices, shifted(): return lax.ppermute(block, axis, route)  26.8 us
    pallas_call x4, Pallas kernels, call(): pl.pallas_call(kernel, grid_spec=pltpu.PrefetchScalarGridSpec(num_scalar_...  25.8 us
    ppermute x7, starting transfers between devices, swapped(): lax.ppermute(block, axis, [(i, i ^ bit) for i in range(lax.axis_size(axis...  14.3 us
    ppermute x7, waiting for transfers between devices, swapped(): lax.ppermute(block, axis, [(i, i ^ bit) for i in range(lax.axis_size(axis...  13.3 us
    all_to_all x2, waiting for transfers between devices, summed(): return jnp.sum(lax.all_to_all(copies, axes, 0, 0, tiled=True), axis=0)  11.3 us
    unnamed x36, local copies, waits for them, and re-layouts  10.8 us
    all_to_all x2, starting transfers between devices, summed(): return jnp.sum(lax.all_to_all(copies, axes, 0, 0, tiled=True), axis=0)  8.06 us
    ppermute x10, waiting for transfers between devices, shifted(): return lax.ppermute(block, axis, route)  7.37 us
  transfers between devices with their start and end apart: 19, of which 8 were waited for; matrix products, arithmetic and copies ran while one was open for 8% of the time, Pallas kernels for 16%

commit v1 on v0

--- a/solution.py
+++ b/solution.py
@@ -5,6 +5,7 @@
 from jax.experimental import pallas as pl
 from jax.experimental.pallas import tpu as pltpu
 from jax.sharding import PartitionSpec as P
+
 
 phase_rate = 0.25
 floor_level = 0.5
@@ -14,6 +15,11 @@
 object_bound = 4.0
 amp_bound = 4.0
 half_range = 32768.0
+vmem_part = 22 * 1024 * 1024
+prep_far = (0, 1, 2, 3, 4, 5, 6)
+exit_far = (0, 1, 2, 3, 5, 8)
+back_far = (0, 1, 2, 6)
+grad_far = (0, 1)
 
 F32 = jnp.float32
 BF16 = jnp.bfloat16
@@ -155,7 +161,7 @@
     size = low_rows.shape[0]
 
     def rows_of(ref):
-        return jnp.where(low_rows, ref[part, :size].astype(F32), ref[part, size:].astype(F32))
+        return jnp.where(low_rows, ref[part, :size].astype(F32), ref[part, size : 2 * size].astype(F32))
 
     halo = jnp.where(left_cols, rows_of(left), rows_of(right))
     return join([halo, rows_of(own)], 1)
@@ -170,10 +176,12 @@
     for ref, term in ((left, to_left), (right, to_right), (own, mine)):
         upper = jnp.where(low_rows, term, zero)
         ref[part, :size] += upper
-        ref[part, size:] += term - upper
-
-
-def prepare_kernel(rows, cols, order, wave, probe, amp, wave_out, probe_out, amp_out, scales, peak):
+        ref[part, size : 2 * size] += term - upper
+
+
+def prepare_kernel(
+    rows, cols, order, wave, probe, amp, strip, wave_out, probe_out, amp_out, first_out, exponents, peak
+):
     position = pl.program_id(0)
     row_at, col_at = rows[position], cols[position]
     parts = wave.shape[1]
@@ -191,6 +199,7 @@
     @pl.when(position == 0)
     def _():
         peak[...] = jnp.zeros_like(peak)
+        first_out[...] = strip[:2]
 
     peak[0:1] = jnp.maximum(peak[0:1], largest)
 
@@ -203,8 +212,11 @@
         chi_bound = size * (2.0 * object_bound * wave_peak + amp_bound)
         second = count * root * wave_peak * chi_bound
         first = count * root * probe_peak * (root * object_bound * chi_bound)
-        tile = lax.broadcasted_iota(jnp.int32, scales.shape, 0)
-        scales[...] = jnp.maximum(jnp.where(tile < 4, second, first), 1e-30) * (1.0 / half_range)
+        shared = count * root * object_bound * (root * object_bound * chi_bound)
+        row = lax.broadcasted_iota(jnp.int32, exponents.shape, 0)
+        bound = jnp.where(row < 8, second, jnp.where(row < 16, first, shared))
+        bound = jnp.maximum(bound, 1e-30)
+        exponents[...] = jnp.ceil(jnp.log2(bound * (1.0 / half_range)))
 
 
 def clear(refs):
@@ -214,13 +226,14 @@
             ref[...] = jnp.zeros_like(ref)
 
 
-def exit_kernel(rows, cols, tables, left_in, own_in, right_in, scales, wave, amp, back, left, own, right):
+def exit_kernel(rows, cols, tables, left_in, own_in, right_in, exponents, wave, amp, back, left, own, right):
     position = pl.program_id(0)
     size = wave.shape[2]
     width = own_in.shape[2]
     half = size // 2
     count = wave.shape[1] // 2
     clear((left, own, right))
+    left[:, 2 * size :] = jnp.broadcast_to(exponents[:16], (2, 16, width))
     low_rows, left_cols = masks(rows[position], cols[position], size, width)
     second_real = patch_of(left_in, own_in, right_in, 0, low_rows, left_cols)
     second_imag = patch_of(left_in, own_in, right_in, 1, low_rows, left_cols)
@@ -262,17 +275,26 @@
         grad_imag = imag if grad_imag is None else grad_imag + imag
         back[0, mode] = second_real * chi_real + second_imag * chi_imag
         back[0, count + mode] = second_real * chi_imag - second_imag * chi_real
-    inverse = 1.0 / scales[0:1, :width]
+    inverse = jnp.exp2(-exponents[0:1])
     scatter(0, grad_real, inverse, left, own, right, low_rows, left_cols)
     scatter(1, grad_imag, inverse, left, own, right, low_rows, left_cols)
 
 
-def back_kernel(rows, cols, tables, scales, back, probe, wave, left, own, right):
+def back_kernel(
+    rows, cols, tables, exponents, right_second, back, probe, wave, left, own, right
+):
     position = pl.program_id(0)
     size = back.shape[2]
     width = own.shape[2]
     count = back.shape[1] // 2
-    clear((left, own, right))
+    clear((left, own))
+
+    @pl.when(position == 0)
+    def _():
+        right[:2, : 2 * size] = jnp.zeros((2, 2 * size, width), F32)
+        right[2:, : 2 * size] = right_second[...]
+        right[:, 2 * size :] = jnp.broadcast_to(exponents[:16], (4, 16, width))
+
     low_rows, left_cols = masks(rows[position], cols[position], size, width)
     fields = [(back[0, mode], back[0, count + mode]) for mode in range(count)]
     plus, minus = fold_rows(fields)
@@ -294,7 +316,7 @@
         term_imag = probe_real * imag - probe_imag * real
         grad_real = term_real if grad_real is None else grad_real + term_real
         grad_imag = term_imag if grad_imag is None else grad_imag + term_imag
-    inverse = 1.0 / scales[4:5, :width]
+    inverse = jnp.exp2(-exponents[8:9])
     scatter(0, grad_real, inverse, left, own, right, low_rows, left_cols)
     scatter(1, grad_imag, inverse, left, own, right, low_rows, left_cols)
 
@@ -334,8 +356,12 @@
     return pl.BlockSpec(tuple(shape), lambda p, *_: zeros)
 
 
-def call(kernel, count, ins, outs, scratch=(), flops=0, transcendentals=0):
+def call(kernel, count, ins, outs, flops, limit=None, scratch=(), far=(), near=(), kept=(), shed=()):
     moved = sum(int(np.prod(a.shape)) * a.dtype.itemsize for a, _ in ins + outs)
+    given = [a for a, _ in ins]
+    for places, space in ((far, pltpu.HBM), (near, pltpu.VMEM)):
+        for at in places:
+            given[at] = pltpu.with_memory_space_constraint(given[at], space)
     return pl.pallas_call(
         kernel,
         grid_spec=pltpu.PrefetchScalarGridSpec(
@@ -345,14 +371,19 @@
             out_specs=[block_of(a.shape) if cut else fixed(a.shape) for a, cut in outs],
             scratch_shapes=list(scratch),
         ),
-        out_shape=[a for a, _ in outs],
-        cost_estimate=pl.CostEstimate(
-            flops=flops, bytes_accessed=moved, transcendentals=transcendentals
+        out_shape=[
+            pltpu.VMEM(a.shape, a.dtype)
+            if at in kept
+            else pltpu.HBM(a.shape, a.dtype)
+            if at in shed
+            else a
+            for at, (a, _) in enumerate(outs)
+        ],
+        cost_estimate=pl.CostEstimate(flops=flops, bytes_accessed=moved, transcendentals=0),
+        compiler_params=pltpu.CompilerParams(
+            dimension_semantics=("arbitrary",), vmem_limit_bytes=limit or vmem_part
         ),
-        compiler_params=pltpu.CompilerParams(
-            dimension_semantics=("arbitrary",), vmem_limit_bytes=48 * 1024 * 1024
-        ),
-    )(*[a for a, _ in ins])
+    )(*given)
 
 
 def shifted(block, axis, distance):
@@ -363,26 +394,6 @@
 
 def swapped(block, axis, bit):
     return lax.ppermute(block, axis, [(i, i ^ bit) for i in range(lax.axis_size(axis))])
-
-
-def halved_sum(block, dim, axis, bit, low):
-    mine = (lax.axis_index(axis) // bit) % 2
-    half = block.shape[dim] // 2
-    pair = (half, 2) if low else (2, half)
-    view = block.reshape(block.shape[:dim] + pair + block.shape[dim + 1 :])
-    at = dim + 1 if low else dim
-    keep = lax.dynamic_index_in_dim(view, mine, at, False)
-    send = lax.dynamic_index_in_dim(view, 1 - mine, at, False)
-    return keep + swapped(send, axis, bit)
-
-
-def bits_of(axis):
-    bit = lax.axis_size(axis) // 2
-    bits = []
-    while bit:
-        bits.append(bit)
-        bit //= 2
-    return bits
 
 
 def summed(values):
@@ -390,6 +401,14 @@
     count = lax.axis_size("group") * lax.axis_size("tile")
     copies = jnp.broadcast_to(values[None], (count,) + values.shape)
     return jnp.sum(lax.all_to_all(copies, axes, 0, 0, tiled=True), axis=0)
+
+
+def lane_row(values):
+    lane = lax.broadcasted_iota(jnp.int32, (128,), 0)
+    row = jnp.zeros((128,), F32)
+    for at, value in enumerate(values):
+        row = jnp.where(lane == at, value, row)
+    return row
 
 
 def shards(object_slices, probe, mid_waves, amplitudes, row_offsets, col_offsets):
@@ -402,13 +421,13 @@
     rows, cols = row_offsets.reshape(count), col_offsets.reshape(count)
     waves = mid_waves.reshape(count, 2 * modes, size, size)
     levels = amplitudes.reshape(count, size, size)
-    first, second = object_slices[:2], object_slices[2:]
-    left_second, right_second = shifted(second, "tile", 1), shifted(second, "tile", -1)
-    left_first, right_first = shifted(first, "tile", 1), shifted(first, "tile", -1)
+    second = object_slices[2:]
+    left_second = shifted(second, "tile", 1)
+    right_second = shifted(second, "tile", -1)
 
     planes = (count, 2 * modes, size, size)
     product = 2 * size**3
-    rolled_waves, rolled_probe, ordered, scales = call(
+    rolled_waves, rolled_probe, ordered, first, exponents = call(
         prepare_kernel,
         count,
         [
@@ -418,19 +437,26 @@
             (waves, 1),
             (probe, 0),
             (levels, 1),
+            (object_slices, 0),
         ],
         [
             (shape_of(planes, BF16), 1),
             (shape_of(planes), 1),
             (shape_of(levels.shape, BF16), 1),
-            (shape_of((8, strip_width)), 0),
+            (shape_of(second.shape, BF16), 0),
+            (shape_of((24, strip_width)), 0),
         ],
         scratch=[pltpu.VMEM((8, size), F32)],
+        far=prep_far,
+        kept=(0, 4),
+        shed=(1, 2),
         flops=count * 2 * product,
     )
-    left_scales, right_scales = shifted(scales, "tile", 1), shifted(scales, "tile", -1)
-    rim = shape_of((2, row_count, strip_width))
-    back, left_rim, own_second, right_rim = call(
+    left_first_strip = shifted(first, "tile", 1)
+    right_first_strip = shifted(first, "tile", -1)
+    strip = shape_of((2, row_count, strip_width))
+    tailed = row_count + 16
+    back, left_rim, own_second, right_second = call(
         exit_kernel,
         count,
         [
@@ -440,87 +466,113 @@
             (left_second, 0),
             (second, 0),
             (right_second, 0),
-            (scales, 0),
+            (exponents, 0),
             (rolled_waves, 1),
             (ordered, 1),
         ],
-        [(shape_of(planes), 1), (rim, 0), (rim, 0), (rim, 0)],
+        [(shape_of(planes), 1), (shape_of((2, tailed, strip_width)), 0), (strip, 0), (strip, 0)],
         flops=count * modes * 24 * product,
-    )
-    from_right_second = shifted(left_rim.astype(jnp.float16), "tile", -1)
-    from_left_second = shifted(right_rim.astype(jnp.float16), "tile", 1)
-    waves_back, left_rim, own_first, right_rim = call(
+        far=exit_far,
+        near=(6, 7),
+        kept=(0, 1, 2, 3),
+    )
+    second_from_right = shifted(left_rim.astype(jnp.float16), "tile", -1)
+    beams, left_first, own_first, right_rim = call(
         back_kernel,
         count,
         [
             (rows, 0),
             (cols, 0),
             (jnp.asarray(back_tables(size)), 0),
-            (scales, 0),
+            (exponents, 0),
+            (right_second, 0),
             (back, 1),
             (rolled_probe, 1),
         ],
-        [(shape_of(planes), 1), (rim, 0), (rim, 0), (rim, 0)],
+        [(shape_of(planes), 1), (strip, 0), (strip, 0), (shape_of((4, tailed, strip_width)), 0)],
         flops=count * modes * 12 * product,
-    )
-    from_right_first = shifted(left_rim.astype(jnp.float16), "tile", -1)
-    from_left_first = shifted(right_rim.astype(jnp.float16), "tile", 1)
+        far=back_far,
+        near=(3, 4, 5),
+        kept=(0, 1, 2, 3),
+    )
+    from_left = shifted(right_rim.astype(jnp.float16), "tile", 1)
+    first_from_right = shifted(left_first.astype(jnp.float16), "tile", -1)
     (grad_probe,) = call(
         probe_kernel,
         count,
         [
             (rows, 0),
             (cols, 0),
-            (left_first, 0),
+            (left_first_strip, 0),
             (first, 0),
-            (right_first, 0),
-            (waves_back, 1),
+            (right_first_strip, 0),
+            (beams, 1),
         ],
         [(shape_of(probe.shape), 0)],
         flops=count * 8 * modes * size * size,
+        far=grad_far,
+        near=(5,),
+        kept=(0,),
     )
 
     share = probe.shape[0] // tiles
     piece = share // groups
-    part = grad_probe.reshape(tiles, groups, piece, size)
-    for bit in reversed(bits_of("group")):
-        part = halved_sum(part, 1, "group", bit, True)
-    for bit in bits_of("tile"):
-        part = halved_sum(part, 0, "tile", bit, False)
-    part = part.reshape(piece, size)
+    chips = groups // 2
+    core = lax.axis_index("group") % 2
+    view = grad_probe.reshape(tiles, chips, 2, piece, size)
+    keep = lax.dynamic_index_in_dim(view, core, 2, False)
+    send = lax.dynamic_index_in_dim(view, 1 - core, 2, False)
+    part = (keep + swapped(send, "group", 1)).swapaxes(0, 1)
+    lines = piece * size // strip_width
+    part = part.reshape(chips * tiles, lines, strip_width) * jnp.exp2(-exponents[16:17])
+    tail = jnp.broadcast_to(exponents[16:24], (chips * tiles, 8, strip_width))
+    part = jnp.concatenate([part, tail], axis=1).astype(jnp.float16)
+    members = [
+        [(2 * chip + side) * tiles + tile for chip in range(chips) for tile in range(tiles)]
+        for side in range(2)
+    ]
+    part = lax.all_to_all(
+        part, ("group", "tile"), 0, 0, axis_index_groups=members, tiled=True
+    )
+    part = jnp.sum(
+        part[:, :lines].astype(F32) * jnp.exp2(part[:, lines : lines + 1].astype(F32)), axis=0
+    )
     probe_squares = jnp.sum(part * part)
+
+    def scale_of(rim, at):
+        row = row_count + 8 * at
+        return jnp.exp2(rim[:, row : row + 1].astype(F32))
+
+    def widened(rim):
+        return rim[:, :row_count].astype(F32)
 
     own_second = (
         own_second
-        + from_right_second.astype(F32) * right_scales[0, 0]
-        + from_left_second.astype(F32) * left_scales[0, 0]
+        + widened(second_from_right) * scale_of(second_from_right, 0)
+        + widened(from_left[2:]) * scale_of(from_left[2:], 0)
     )
     own_first = (
         own_first
-        + from_right_first.astype(F32) * right_scales[4, 0]
-        + from_left_first.astype(F32) * left_scales[4, 0]
+        + widened(first_from_right) * scale_of(second_from_right, 1)
+        + widened(from_left[:2]) * scale_of(from_left[:2], 1)
     )
     own_grad = jnp.concatenate([own_first, own_second])
     object_squares = jnp.sum(own_grad * own_grad)
-    object_total = summed(object_squares.reshape(1))[0]
-    probe_total = summed(probe_squares.reshape(1))[0]
+    totals = summed(lane_row([object_squares, probe_squares]))
+    object_total, probe_total = totals[0], totals[1]
     object_count = 4 * row_count * strip_width * groups * tiles
-    object_rms = jnp.sqrt(object_total / object_count + epsilon)
-    object_new = object_slices.astype(F32) - object_step * own_grad / object_rms
-
-    whole = part
-    for bit in reversed(bits_of("group")):
-        other = swapped(whole, "group", bit)
+    object_factor = object_step / jnp.sqrt(object_total / object_count + epsilon)
+    object_new = object_slices.astype(F32) - object_factor * own_grad
+
+    part = part.reshape(piece, size)
+    for bit in (1, 2):
+        other = swapped(part, "group", bit)
         mine = (lax.axis_index("group") // bit) % 2
-        whole = jnp.where(
-            mine == 0,
-            jnp.concatenate([whole, other]),
-            jnp.concatenate([other, whole]),
-        )
-    probe_rms = jnp.sqrt(probe_total / probe.size + epsilon)
+        part = jnp.where(mine == 0, jnp.concatenate([part, other]), jnp.concatenate([other, part]))
+    probe_factor = probe_step / jnp.sqrt(probe_total / probe.size + epsilon)
     start_row = lax.axis_index("tile") * share
     probe_rows = lax.dynamic_slice_in_dim(probe, start_row, share, 0)
-    probe_new = probe_rows - probe_step * whole / probe_rms
+    probe_new = probe_rows - probe_factor * part
     return (object_new, probe_new)
 
 

time: 138 us -> 101 us (0.73)
  waiting for transfers between devices: 31.9 us -> 17.7 us
  local copies, waits for them, and re-layouts: 17.1 us -> 3.16 us
  starting transfers between devices: 49.2 us -> 38.5 us
  Pallas kernels: 25.8 us -> 28.7 us
    ppermute x7 -> x3, starting transfers between devices: 14.3 us -> 1.05 us  [swapped(): lax.ppermute(block, axis, [(i, i ^ bit) for i in range(lax.axis_size(axis...]
    ppermute x7 -> x3, waiting for transfers between devices: 13.3 us -> 1.9 us  [swapped(): lax.ppermute(block, axis, [(i, i ^ bit) for i in range(lax.axis_size(axis...]
    unnamed x36 -> x6, local copies, waits for them, and re-layouts: 10.8 us -> 0.79 us
    all_to_all x0 -> x1, starting transfers between devices: none -> 8.35 us  [shards(): lax.all_to_all(part, ('group', 'tile'), 0, 0, axis_index_groups=members,...]
    ppermute x10 -> x7, starting transfers between devices: 26.8 us -> 21.6 us  [shifted(): return lax.ppermute(block, axis, route)]
    all_to_all x2 -> x1, waiting for transfers between devices: 11.3 us -> 6.69 us  [summed(): return jnp.sum(lax.all_to_all(copies, axes, 0, 0, tiled=True), axis=0)]
    add x6 -> x1, other arithmetic: 4.96 us -> 1.41 us  [shards(): own_first + widened(first_from_right) * scale_of(second_from_right, 1)]
    pallas_call x4, Pallas kernels: 25.8 us -> 28.7 us  [call(): pl.pallas_call(kernel, grid_spec=pltpu.PrefetchScalarGridSpec(num_scalar_...]
  transfers between devices with their start and end apart: 19 -> 12, of which waited for: 8 -> 3; matrix products, arithmetic and copies ran while one was open for 8% -> 7% of each run, Pallas kernels for 16% -> 29%
where the time goes in v1:
time: 101 us
  starting transfers between devices  38.5 us (38%)
  Pallas kernels  28.7 us (28%)
  waiting for transfers between devices  17.7 us (18%)
  other arithmetic  10.1 us (10%)
  local copies, waits for them, and re-layouts  3.16 us (3%)
  between operations  2.38 us (2%)
    pallas_call x4, Pallas kernels, call(): pl.pallas_call(kernel, grid_spec=pltpu.PrefetchScalarGridSpec(num_scalar_...  28.7 us
    ppermute x7, starting transfers between devices, shifted(): return lax.ppermute(block, axis, route)  21.6 us
    ppermute x7, waiting for transfers between devices, shifted(): return lax.ppermute(block, axis, route)  9.09 us
    all_to_all x1, starting transfers between devices, shards(): lax.all_to_all(part, ('group', 'tile'), 0, 0, axis_index_groups=members,...  8.35 us
    all_to_all x1, starting transfers between devices, summed(): return jnp.sum(lax.all_to_all(copies, axes, 0, 0, tiled=True), axis=0)  7.52 us
    all_to_all x1, waiting for transfers between devices, summed(): return jnp.sum(lax.all_to_all(copies, axes, 0, 0, tiled=True), axis=0)  6.69 us
  transfers between devices with their start and end apart: 12, of which 3 were waited for; matrix products, arithmetic and copies ran while one was open for 7% of the time, Pallas kernels for 29%

profile of v1, /device:TPU:0, one launch (start us, length us, event | category | flops | bytes accessed | tf_op | source)
XLA Modules:
  0.0 100.6 jit_solution(17834892626679662894)
XLA Ops:
  0.6 1.0 slice.50.own_in
  1.6 4.9 %collective-permute-start.2 = (bf16[2,512,128]{2,1,0:T(8,128)(2,1)S(1)}, bf16[2,512,128]{2,1,0:T(8,128)(2,1)S(1)}, u32[]{:S(2)}, u32[]{:S(2)}) collective-permute-start(bf16[2,512,128]{2,1,0:T(8,128)(2,1)S(1)} %slice.50.own_in), channel_id=1, source_target_pairs={{0,1},{1,2},{2,3},{3,4},{4,5},{5,6},{6,7},{8,9},{9,10},{10,11},{11... | collective-permute-start | bytes 786440 | tf_op jit(solution)/shard_map/ppermute | solution.py:392
  6.5 1.3 %collective-permute-start.3 = (bf16[2,512,128]{2,1,0:T(8,128)(2,1)S(1)}, bf16[2,512,128]{2,1,0:T(8,128)(2,1)S(1)}, u32[]{:S(2)}, u32[]{:S(2)}) collective-permute-start(bf16[2,512,128]{2,1,0:T(8,128)(2,1)S(1)} %slice.50.own_in), channel_id=1, source_target_pairs={{1,0},{2,1},{3,2},{4,3},{5,4},{6,5},{7,6},{9,8},{10,9},{11,10},{12... | collective-permute-start | bytes 786440 | tf_op jit(solution)/shard_map/ppermute | solution.py:392
  7.8 6.8 %shard_map.104 = (bf16[3,4,256,256]{3,2,1,0:T(8,128)(2,1)S(1)}, f32[3,4,256,256]{3,2,1,0:T(8,128)}, bf16[3,256,256]{2,1,0:T(8,128)(2,1)}, bf16[2,512,128]{2,1,0:T(8,128)(2,1)S(1)}, f32[24,128]{1,0:T(8,128)S(1)}) custom-call(s32[3]{0:T(128)} %bitcast.36, s32[3]{0:T(128)} %bitcast.40, bf16[2,256,256]{2,1,0:T(8,128)(2,1)} %constant.93.clone.order, ...), custom_call_target="tpu_custom_call" | custom-call | flops 201326592 | bytes 9187352 | tf_op jit(solution)/shard_map/pallas_call | solution.py:365
  14.6 4.6 %collective-permute-start = (bf16[2,512,128]{2,1,0:T(8,128)(2,1)S(1)}, bf16[2,512,128]{2,1,0:T(8,128)(2,1)S(1)}, u32[]{:S(2)}, u32[]{:S(2)}) collective-permute-start(bf16[2,512,128]{2,1,0:T(8,128)(2,1)S(1)} %get-tuple-element.15.own_in), channel_id=1, source_target_pairs={{0,1},{1,2},{2,3},{3,4},{4,5},{5,6},{6,7},{8,9},{9,10},{10,11},{11... | collective-permute-start | bytes 786440 | tf_op jit(solution)/shard_map/ppermute | solution.py:392
  19.2 1.3 %collective-permute-start.1 = (bf16[2,512,128]{2,1,0:T(8,128)(2,1)S(1)}, bf16[2,512,128]{2,1,0:T(8,128)(2,1)S(1)}, u32[]{:S(2)}, u32[]{:S(2)}) collective-permute-start(bf16[2,512,128]{2,1,0:T(8,128)(2,1)S(1)} %get-tuple-element.15.own_in), channel_id=1, source_target_pairs={{1,0},{2,1},{3,2},{4,3},{5,4},{6,5},{7,6},{9,8},{10,9},{11,10},{12... | collective-permute-start | bytes 786440 | tf_op jit(solution)/shard_map/ppermute | solution.py:392
  20.5 0.0 collective-permute-done.2.left_in
  20.5 0.0 collective-permute-done.3.right_in
  20.6 0.7 copy-done.2
  21.3 0.0 copy-done.1
  21.3 11.0 %shard_map.105 = (f32[3,4,256,256]{3,2,1,0:T(8,128)S(1)}, f32[2,528,128]{2,1,0:T(8,128)S(1)}, f32[2,512,128]{2,1,0:T(8,128)S(1)}, f32[2,512,128]{2,1,0:T(8,128)S(1)}) custom-call(s32[3]{0:T(128)} %bitcast.37, s32[3]{0:T(128)} %bitcast.41, bf16[4,2,256,256]{3,2,1,0:T(8,128)(2,1)} %constant.94.clone.tables, bf16[2,512,128]{2,1,0:T(8,128)(2,1)} %copy-done.1, ...), custom_call_target="tpu_custom_call" | custom-call | flops 4831838208 | bytes 8548376 | tf_op jit(solution)/shard_map/pallas_call | solution.py:365
  32.4 1.3 %collective-permute-start.6 = (f16[2,528,128]{2,1,0:T(8,128)(2,1)S(1)}, f16[2,528,128]{2,1,0:T(8,128)(2,1)}, u32[]{:S(2)}, u32[]{:S(2)}) collective-permute-start(f16[2,528,128]{2,1,0:T(8,128)(2,1)S(1)} %convert_element_type.48), channel_id=1, source_target_pairs={{1,0},{2,1},{3,2},{4,3},{5,4},{6,5},{7,6},{9,8},{10,9},{11,10},{12... | collective-permute-start | bytes 811016 | tf_op jit(solution)/shard_map/ppermute | solution.py:392
  33.7 6.7 %shard_map.106 = (f32[3,4,256,256]{3,2,1,0:T(8,128)S(1)}, f32[2,512,128]{2,1,0:T(8,128)S(1)}, f32[2,512,128]{2,1,0:T(8,128)S(1)}, f32[4,528,128]{2,1,0:T(8,128)S(1)}) custom-call(s32[3]{0:T(128)} %bitcast.38, s32[3]{0:T(128)} %bitcast.42, bf16[4,2,256,256]{3,2,1,0:T(8,128)(2,1)} %constant.95.clone.tables, f32[24,128]{1,0:T(8,128)S(1)} %get-tuple-element.16.exponents, ...), custom_call_target="tpu_custom_call" | custom-call | flops 2415919104 | bytes 13152280 | tf_op jit(solution)/shard_map/pallas_call | solution.py:365
  40.4 0.0 collective-permute-done.left_in
  40.4 0.0 collective-permute-done.1.right_in
  40.4 4.2 %shard_map.107 = f32[1024,256]{1,0:T(8,128)S(1)} custom-call(s32[3]{0:T(128)} %bitcast.39, s32[3]{0:T(128)} %bitcast.43, bf16[2,512,128]{2,1,0:T(8,128)(2,1)S(1)} %collective-permute-done.left_in, bf16[2,512,128]{2,1,0:T(8,128)(2,1)S(1)} %get-tuple-element.15.own_in, bf16[2,512,128]{2,1,0:T(8,128)(2,1)S(1)} %collective-permute-done.1.right_in, ...), custom_call_target="tpu_custom_call" | custom-call | flops 3145728 | bytes 4980760 | tf_op jit(solution)/shard_map/pallas_call | solution.py:365
  44.6 0.1 constant_dynamic-slice_fusion.1
  44.8 0.1 collective-permute-start.4
  44.9 0.8 convert_element_type.46
  45.6 1.3 %collective-permute-start.5 = (f16[2,512,128]{2,1,0:T(8,128)(2,1)}, f16[2,512,128]{2,1,0:T(8,128)(2,1)}, u32[]{:S(2)}, u32[]{:S(2)}) collective-permute-start(f16[2,512,128]{2,1,0:T(8,128)(2,1)} %convert_element_type.46), channel_id=1, source_target_pairs={{1,0},{2,1},{3,2},{4,3},{5,4},{6,5},{7,6},{9,8},{10,9},{11,10},{12... | collective-permute-start | bytes 786440 | tf_op jit(solution)/shard_map/ppermute | solution.py:392
  46.9 0.1 convert_element_type.50
  47.0 7.0 %collective-permute-start.7 = (f16[4,528,128]{2,1,0:T(8,128)(2,1)S(1)}, f16[4,528,128]{2,1,0:T(8,128)(2,1)}, u32[]{:S(2)}, u32[]{:S(2)}) collective-permute-start(f16[4,528,128]{2,1,0:T(8,128)(2,1)S(1)} %convert_element_type.50), channel_id=1, source_target_pairs={{0,1},{1,2},{2,3},{3,4},{4,5},{5,6},{6,7},{8,9},{9,10},{10,11},{11... | collective-permute-start | bytes 1622024 | tf_op jit(solution)/shard_map/ppermute | solution.py:392
  54.0 0.0 collective-permute-done.6
  54.0 0.7 fusion.12
  54.7 0.1 fusion
  54.8 0.1 multiply_convert_fusion
  54.9 0.0 copy-start
  54.9 0.8 pad_maximum_fusion.1
  55.7 8.3 %all-to-all-start = ((f16[16,72,128]{2,1,0:T(8,128)(2,1)}), f16[16,72,128]{2,1,0:T(8,128)(2,1)S(1)}, u32[]{:S(2)}, u32[]{:S(2)}) async-start(f16[16,72,128]{2,1,0:T(8,128)(2,1)} %pad_maximum_fusion.1), calls=%async_computation | async-start | bytes 589824 | tf_op jit(solution)/shard_map/all_to_all | solution.py:534
  64.1 9.1 %collective-permute-done.7 = f16[4,528,128]{2,1,0:T(8,128)(2,1)} collective-permute-done((f16[4,528,128]{2,1,0:T(8,128)(2,1)S(1)}, f16[4,528,128]{2,1,0:T(8,128)(2,1)}, u32[]{:S(2)}, u32[]{:S(2)}) %collective-permute-start.7) | collective-permute-done | bytes 540704 | tf_op jit(solution)/shard_map/ppermute | solution.py:392
  73.1 0.7 fusion.10
  73.8 0.0 collective-permute-done.5
  73.8 1.4 %multiply_add_fusion.1 = (f32[2,512,128]{2,1,0:T(8,128)S(1)}, f32[2,512,128]{2,1,0:T(8,128)S(1)}) fusion(f32[2,512,128]{2,1,0:T(8,128)S(1)} %get-tuple-element.23, f16[2,512,128]{2,1,0:T(8,128)(2,1)} %collective-permute-done.5, f16[4,528,128]{2,1,0:T(8,128)(2,1)} %collective-permute-done.7, f32[2,128]{1,0:T(2,128)S(1)} %bitcast.34, f32[2,128]{1,0:T(2,128)S(1)} %bitcast.32, ...), kind=kLoop, calls=%fused_computation.7 | loop fusion | flops 1572864 | bytes 3149824 | tf_op jit(solution)/shard_map/add | solution.py:555
  75.3 0.9 multiply_reduce_fusion
  76.1 0.0 all-to-all-done
  76.2 0.1 multiply_reduce_fusion.1
  76.2 0.6 multiply_reduce_fusion.2
  76.8 1.3 %compare_select_fusion.1 = f32[128]{0:T(128)S(1)} fusion(f32[]{:T(128)} %multiply_reduce_fusion, f32[]{:T(128)} %multiply_reduce_fusion.2), kind=kLoop, calls=%fused_computation.21 | loop fusion | flops 512 | bytes 520 | tf_op jit(solution)/shard_map/jit(_where)/select_n | solution.py:410
  78.1 0.6 broadcast_in_dim.24
  78.7 7.5 %all-to-all-start.1 = ((f32[32,1,128]{2,1,0:T(1,128)}), f32[32,1,128]{2,1,0:T(1,128)S(1)}, u32[]{:S(2)}, u32[]{:S(2)}) async-start(f32[32,1,128]{2,1,0:T(1,128)} %broadcast_in_dim.24), calls=%async_computation.1 | async-start | bytes 32768 | tf_op jit(solution)/shard_map/all_to_all | solution.py:403
  86.3 0.3 collective-permute-start.8
  86.6 6.7 %all-to-all-done.1 = f32[32,1,128]{2,1,0:T(1,128)S(1)} async-done(((f32[32,1,128]{2,1,0:T(1,128)}), f32[32,1,128]{2,1,0:T(1,128)S(1)}, u32[]{:S(2)}, u32[]{:S(2)}) %all-to-all-start.1) | async-done | bytes 16416 | tf_op jit(solution)/shard_map/all_to_all | solution.py:403
  93.4 0.6 fusion.13
  94.6 0.0 collective-permute-done.8
  94.7 0.7 collective-permute-start.9
  95.3 1.1 %multiply_subtract_fusion = f32[4,512,128]{2,1,0:T(8,128)} fusion(bf16[4,512,128]{2,1,0:T(8,128)(2,1)S(1)} %copy-done, f32[2,512,128]{2,1,0:T(8,128)S(1)} %get-tuple-element.31, f32[2,512,128]{2,1,0:T(8,128)S(1)} %get-tuple-element.30, f32[]{:T(128)} %bitcast.15), kind=kLoop, calls=%fused_computation.1 | loop fusion | flops 1048576 | bytes 2621444 | tf_op jit(solution)/shard_map/sub | solution.py:565
  97.1 1.9 %collective-permute-done.9 = f32[64,256]{1,0:T(8,128)S(1)} collective-permute-done((f32[64,256]{1,0:T(8,128)S(1)}, f32[64,256]{1,0:T(8,128)S(1)}, u32[]{:S(2)}, u32[]{:S(2)}) %collective-permute-start.9) | collective-permute-done | bytes 65568 | tf_op jit(solution)/shard_map/ppermute | solution.py:396
  99.0 1.6 %fusion.2 = f32[128,256]{1,0:T(8,128)} fusion(f32[64,256]{1,0:T(8,128)S(1)} %collective-permute-done.9, f32[64,256]{1,0:T(8,128)S(1)} %maximum_select_fusion.1, f32[1024,256]{1,0:T(8,128)} %probe.1, s32[]{:T(128)S(6)} %select_n.64, f32[]{:T(128)} %bitcast.16, pred[]{:T(512)S(6)} %eq.34), kind=kLoop, calls=%fused_computation.13 | loop fusion | flops 163840 | bytes 393225 | tf_op jit(solution)/shard_map/sub | solution.py:575
  (14 shorter events, 0.2 us)
Async XLA Ops:
  1.6 18.9 %collective-permute-start.2 = (bf16[2,512,128]{2,1,0:T(8,128)(2,1)S(1)}, bf16[2,512,128]{2,1,0:T(8,128)(2,1)S(1)}, u32[]{:S(2)}, u32[]{:S(2)}) collective-permute-start(bf16[2,512,128]{2,1,0:T(8,128)(2,1)S(1)} %slice.50.own_in), channel_id=1, source_target_pairs={{0,1},{1,2},{2,3},{3,4},{4,5},{5,6},{6,7},{8,9},{9,10},{10,11},{11... | collective-permute-start | bytes 786440 | tf_op jit(solution)/shard_map/ppermute | solution.py:392
  6.5 14.0 %collective-permute-start.3 = (bf16[2,512,128]{2,1,0:T(8,128)(2,1)S(1)}, bf16[2,512,128]{2,1,0:T(8,128)(2,1)S(1)}, u32[]{:S(2)}, u32[]{:S(2)}) collective-permute-start(bf16[2,512,128]{2,1,0:T(8,128)(2,1)S(1)} %slice.50.own_in), channel_id=1, source_target_pairs={{1,0},{2,1},{3,2},{4,3},{5,4},{6,5},{7,6},{9,8},{10,9},{11,10},{12... | collective-permute-start | bytes 786440 | tf_op jit(solution)/shard_map/ppermute | solution.py:392
  14.6 25.7 %collective-permute-start = (bf16[2,512,128]{2,1,0:T(8,128)(2,1)S(1)}, bf16[2,512,128]{2,1,0:T(8,128)(2,1)S(1)}, u32[]{:S(2)}, u32[]{:S(2)}) collective-permute-start(bf16[2,512,128]{2,1,0:T(8,128)(2,1)S(1)} %get-tuple-element.15.own_in), channel_id=1, source_target_pairs={{0,1},{1,2},{2,3},{3,4},{4,5},{5,6},{6,7},{8,9},{9,10},{10,11},{11... | collective-permute-start | bytes 786440 | tf_op jit(solution)/shard_map/ppermute | solution.py:392
  19.2 21.2 %collective-permute-start.1 = (bf16[2,512,128]{2,1,0:T(8,128)(2,1)S(1)}, bf16[2,512,128]{2,1,0:T(8,128)(2,1)S(1)}, u32[]{:S(2)}, u32[]{:S(2)}) collective-permute-start(bf16[2,512,128]{2,1,0:T(8,128)(2,1)S(1)} %get-tuple-element.15.own_in), channel_id=1, source_target_pairs={{1,0},{2,1},{3,2},{4,3},{5,4},{6,5},{7,6},{9,8},{10,9},{11,10},{12... | collective-permute-start | bytes 786440 | tf_op jit(solution)/shard_map/ppermute | solution.py:392
  20.5 0.8 copy-start.1
  20.5 0.8 copy-start.2
  32.4 21.6 %collective-permute-start.6 = (f16[2,528,128]{2,1,0:T(8,128)(2,1)S(1)}, f16[2,528,128]{2,1,0:T(8,128)(2,1)}, u32[]{:S(2)}, u32[]{:S(2)}) collective-permute-start(f16[2,528,128]{2,1,0:T(8,128)(2,1)S(1)} %convert_element_type.48), channel_id=1, source_target_pairs={{1,0},{2,1},{3,2},{4,3},{5,4},{6,5},{7,6},{9,8},{10,9},{11,10},{12... | collective-permute-start | bytes 811016 | tf_op jit(solution)/shard_map/ppermute | solution.py:392
  44.8 9.9 %collective-permute-start.4 = (f32[8,2,32,256]{3,2,0,1:T(8,128)S(1)}, f32[8,2,32,256]{3,2,0,1:T(8,128)S(1)}, u32[]{:S(2)}, u32[]{:S(2)}) collective-permute-start(f32[8,2,32,256]{3,2,0,1:T(8,128)S(1)} %bitcast.28), channel_id=1, source_target_pairs={{0,8},{8,0},{16,24},{24,16},{1,9},{9,1},{17,25},{25,17},{2,10},{10... | collective-permute-start | bytes 1572872 | tf_op jit(solution)/shard_map/ppermute | solution.py:396
  45.6 28.2 %collective-permute-start.5 = (f16[2,512,128]{2,1,0:T(8,128)(2,1)}, f16[2,512,128]{2,1,0:T(8,128)(2,1)}, u32[]{:S(2)}, u32[]{:S(2)}) collective-permute-start(f16[2,512,128]{2,1,0:T(8,128)(2,1)} %convert_element_type.46), channel_id=1, source_target_pairs={{1,0},{2,1},{3,2},{4,3},{5,4},{6,5},{7,6},{9,8},{10,9},{11,10},{12... | collective-permute-start | bytes 786440 | tf_op jit(solution)/shard_map/ppermute | solution.py:392
  47.0 26.2 %collective-permute-start.7 = (f16[4,528,128]{2,1,0:T(8,128)(2,1)S(1)}, f16[4,528,128]{2,1,0:T(8,128)(2,1)}, u32[]{:S(2)}, u32[]{:S(2)}) collective-permute-start(f16[4,528,128]{2,1,0:T(8,128)(2,1)S(1)} %convert_element_type.50), channel_id=1, source_target_pairs={{0,1},{1,2},{2,3},{3,4},{4,5},{5,6},{6,7},{8,9},{9,10},{10,11},{11... | collective-permute-start | bytes 1622024 | tf_op jit(solution)/shard_map/ppermute | solution.py:392
  54.9 40.4 %copy-start = (bf16[4,512,128]{2,1,0:T(8,128)(2,1)S(1)}, bf16[4,512,128]{2,1,0:T(8,128)(2,1)}, u32[]{:S(2)}) copy-start(bf16[4,512,128]{2,1,0:T(8,128)(2,1)} %strip.1) | copy-start | bytes 1572868
  55.7 20.4 %all-to-all-start = ((f16[16,72,128]{2,1,0:T(8,128)(2,1)}), f16[16,72,128]{2,1,0:T(8,128)(2,1)S(1)}, u32[]{:S(2)}, u32[]{:S(2)}) async-start(f16[16,72,128]{2,1,0:T(8,128)(2,1)} %pad_maximum_fusion.1), calls=%async_computation | async-start | bytes 589824 | tf_op jit(solution)/shard_map/all_to_all | solution.py:534
  78.7 14.6 %all-to-all-start.1 = ((f32[32,1,128]{2,1,0:T(1,128)}), f32[32,1,128]{2,1,0:T(1,128)S(1)}, u32[]{:S(2)}, u32[]{:S(2)}) async-start(f32[32,1,128]{2,1,0:T(1,128)} %broadcast_in_dim.24), calls=%async_computation.1 | async-start | bytes 32768 | tf_op jit(solution)/shard_map/all_to_all | solution.py:403
  86.3 8.3 %collective-permute-start.8 = (f32[32,256]{1,0:T(8,128)S(1)}, f32[32,256]{1,0:T(8,128)S(1)}, u32[]{:S(2)}, u32[]{:S(2)}) collective-permute-start(f32[32,256]{1,0:T(8,128)S(1)} %reshape.60), channel_id=1, source_target_pairs={{0,8},{8,0},{16,24},{24,16},{1,9},{9,1},{17,25},{25,17},{2,10},{10... | collective-permute-start | bytes 98312 | tf_op jit(solution)/shard_map/ppermute | solution.py:396
  94.7 4.3 %collective-permute-start.9 = (f32[64,256]{1,0:T(8,128)S(1)}, f32[64,256]{1,0:T(8,128)S(1)}, u32[]{:S(2)}, u32[]{:S(2)}) collective-permute-start(f32[64,256]{1,0:T(8,128)S(1)} %maximum_select_fusion.1), channel_id=1, source_target_pairs={{0,16},{8,24},{16,0},{24,8},{1,17},{9,25},{17,1},{25,9},{2,18},{10... | collective-permute-start | bytes 196616 | tf_op jit(solution)/shard_map/ppermute | solution.py:396
